TPU v7x, 256 devices: a whole 4x4x8 slice. The times are simulated.
256 devices in a mesh: chan: 4 (over x), mset: 8 (over y, core), blk: 8 (over z).
Axes of the slice: x: 4, y: 4, z: 8, core: 2. Of those that a mesh axis runs over, the one named last changes fastest.
Arguments:
- harmonics: bfloat16 [2, 3, 64, 1536], P(None, None, ('mset', 'blk'), 'chan'), may hold values from -6 to 6
- mixing: float32 [12, 3], replicated, may hold values from 0.2 to 1.2
- beam_window: float32 [12, 1536], P(None, 'chan'), may hold values from 0.2 to 1
- prior_inv: float32 [3, 1536], P(None, 'chan'), may hold values from 0.3 to 3
- legendre: bfloat16 [64, 1536, 8192], P(('mset', 'blk'), 'chan'), may hold values from -0.15625 to 0.15625
- inv_noise: bfloat16 [12, 8192, 8192], P('chan', ('mset', 'blk')), may hold values from 0.0099487305 to 0.099609375
- mode_index: int32 [64], replicated, may hold values from 0 to 1535, as said below
- cycle_pixels: int32 [12], replicated, may hold values from 2048 to 8192, as said below
Outputs:
- applied: float32 [2, 3, 64, 1536], P(None, None, ('mset', 'blk'), 'chan')
Inputs may be any that keep to these rules, and one draw needn't show every extreme that they name: `mode_index`: distinct values; 0 and 1535 are always among them. `cycle_pixels`: each value is 2048, 4096 or 8192; every draw holds both the smallest and the largest.
All inputs are finite; a program needn't handle non-finite values.
Results may differ from a plain program's by a relative error of at most 0.005.
Values may be sent and summed in bfloat16 or wider, within the bound.
No kernel may reach another device: no remote copies, remote signals or barrier semaphores. Data moves between devices by JAX's collectives and lax.ppermute only.
A program may use at most 128 MiB of HBM per device.

v0:
```python
import math
import jax
import jax.numpy as jnp
from jax import lax
from jax.sharding import PartitionSpec as P


def make_table(mode_index, npix, pixels, mode_count):
    fine_width = 128
    coarse_count = pixels // fine_width
    twice = 2 * npix
    coarse_idx = jnp.arange(coarse_count)
    fine_idx = jnp.arange(fine_width)
    coarse_res = mode_index[:, None] * (2 * fine_width * coarse_idx)[None, :] % twice
    fine_res = mode_index[:, None] * (2 * fine_idx + 1)[None, :] % twice
    scale = jnp.pi / npix.astype(jnp.float32)
    coarse_phase = scale * coarse_res.astype(jnp.float32)
    fine_phase = scale * fine_res.astype(jnp.float32)
    coarse_cos = jnp.cos(coarse_phase)[:, :, None]
    coarse_sin = jnp.sin(coarse_phase)[:, :, None]
    fine_cos = jnp.cos(fine_phase)[:, None, :]
    fine_sin = jnp.sin(fine_phase)[:, None, :]
    cos_full = (coarse_cos * fine_cos - coarse_sin * fine_sin).reshape(mode_count, pixels)
    sin_full = (coarse_sin * fine_cos + coarse_cos * fine_sin).reshape(mode_count, pixels)
    pix_index = jnp.arange(pixels)
    inside = pix_index[None, :] < npix
    weight = jnp.where(mode_index == 0, 1.0, 2.0).astype(jnp.float32)[:, None] / math.sqrt(
        2 * mode_count
    )
    cos_part = jnp.where(inside, weight * cos_full, 0.0)
    sin_part = jnp.where(inside, -weight * sin_full, 0.0)
    return jnp.concatenate([cos_part, sin_part], axis=0).astype(jnp.bfloat16)


def on_device(
    harmonics, mixing, beam_window, prior_inv, legendre, inv_noise, mode_index, cycle_pixels
):
    chan_count = lax.axis_size("chan")
    chan_pos = lax.axis_index("chan")
    chan_slots = inv_noise.shape[0]
    cycle_dev = inv_noise.shape[1]
    pixels = inv_noise.shape[2]
    channels = mixing.shape[0]
    mode_shard = legendre.shape[0]
    local_deg = legendre.shape[1]
    mode_count = mode_index.shape[0]
    total_deg = local_deg * chan_count
    degrees = chan_pos * local_deg + jnp.arange(local_deg)
    band_limit = total_deg * cycle_pixels // pixels - 1
    filter_bank = jnp.where(degrees[None, :] <= band_limit[:, None], beam_window, 0.0)
    coeffs = harmonics.astype(jnp.float32)
    mixture = (
        jnp.sum(mixing[:, None, :, None, None] * coeffs[None], axis=2)
        * filter_bank[:, None, None, :]
    )
    channel_harmonic_coeffs = mixture.astype(jnp.bfloat16).reshape(
        2 * channels, mode_shard, local_deg
    )
    partial_value = jnp.einsum(
        "ijn,jnw->ijw", channel_harmonic_coeffs, legendre, preferred_element_type=jnp.float32
    )
    reduced_sum = lax.psum_scatter(
        partial_value.astype(jnp.bfloat16), "chan", scatter_dimension=0, tiled=True
    )
    cycle_data = lax.all_to_all(
        reduced_sum, ("mset", "blk"), split_axis=2, concat_axis=1, tiled=True
    )
    own_pixels = lax.dynamic_slice_in_dim(cycle_pixels, chan_pos * chan_slots, chan_slots)
    tables = jax.vmap(lambda npix: make_table(mode_index, npix, pixels, mode_count))(own_pixels)
    spectra = cycle_data.reshape(chan_slots, 2 * mode_count, cycle_dev)
    sky_map = jnp.einsum("cnr,cnp->crp", spectra, tables, preferred_element_type=jnp.float32)
    noisy_map = (sky_map * inv_noise).astype(jnp.bfloat16)
    mode_spectra = jnp.einsum("cnp,crp->cnr", tables, noisy_map, preferred_element_type=jnp.float32)
    mode_spectra = mode_spectra.astype(jnp.bfloat16).reshape(2 * chan_slots, mode_count, cycle_dev)
    returned = lax.all_to_all(
        mode_spectra, ("mset", "blk"), split_axis=1, concat_axis=2, tiled=True
    )
    collected_rows = lax.all_gather(returned, "chan", axis=0, tiled=True)
    harmonic_back = jnp.einsum(
        "ogb,gfb->ogf", collected_rows, legendre, preferred_element_type=jnp.float32
    )
    harmonic_back = harmonic_back.reshape(channels, 2, mode_shard, local_deg)
    weighted = harmonic_back * filter_bank[:, None, None, :]
    transposed = jnp.einsum("ck,ciml->ikml", mixing, weighted, precision=lax.Precision.HIGHEST)
    return prior_inv[None, :, None, :] * coeffs + transposed


def solution(mesh):
    placed = (
        P(None, None, ("mset", "blk"), "chan"),
        P(),
        P(None, "chan"),
        P(None, "chan"),
        P(("mset", "blk"), "chan", None),
        P("chan", ("mset", "blk"), None),
        P(),
        P(),
    )
    return jax.shard_map(
        on_device,
        mesh=mesh,
        in_specs=placed,
        out_specs=P(None, None, ("mset", "blk"), "chan"),
        check_vma=False,
    )
```

profile of v0, /device:TPU:8, one launch (start us, length us, event | category | flops | bytes accessed | tf_op | source)
XLA Modules:
  0.0 190.6 jit_solution(135521996411559418)
XLA Ops:
  0.0 0.7 fusion.28
  0.7 0.7 convert_bitcast_fusion
  1.4 0.8 copy.33
  2.2 0.1 multiply_reduce_fusion
  2.3 0.8 compare_select_fusion
  3.2 3.7 %fusion.1 = bf16[24,1,8192]{2,0,1:T(8,128)(2,1)S(1)} fusion(bf16[24,384]{1,0:T(8,128)(2,1)S(1)} %convert_element_type.71, bf16[1,384,8192]{2,1,0:T(8,128)(2,1)} %param.12), kind=kOutput, calls=%fused_computation.2 | convolution fusion | flops 151191552 | bytes 6703104 | tf_op jit(solution)/shard_map/ijn,jnw->ijw/dot_general | solution.py:59
  6.9 13.8 %fusion = bf16[8,8192]{1,0:T(8,128)(2,1)S(1)} fusion(bf16[24,1,8192]{2,0,1:T(8,128)(2,1)S(1)} %fusion.1), kind=kCustom, calls=%all-reduce-scatter | all-reduce-scatter fusion | flops 262145 | bytes 525312
  20.8 3.6 %collective-permute-start = (bf16[6,8192]{1,0:T(8,128)(2,1)S(1)}, bf16[6,8192]{1,0:T(8,128)(2,1)S(1)}, u32[]{:S(2)}, u32[]{:S(2)}) collective-permute-start(bf16[6,8192]{1,0:T(8,128)(2,1)S(1)} %slice), channel_id=1, source_target_pairs={{0,64},{64,128},{128,192},{1,65},{65,129},{129,193},{2,66},{66,130... | collective-permute-start | bytes 294920
  24.8 1.4 fusion.16
  26.2 1.4 fusion.20
  27.6 7.1 %multiply_subtract_fusion = (f32[3,64,64,128]{3,2,1,0:T(8,128)}, f32[3,64,64,128]{3,2,1,0:T(8,128)}) fusion(f32[3,64,128]{2,1,0:T(8,128)S(1)} %get-tuple-element.12, f32[3,64,64]{2,1,0:T(8,128)S(1)} %get-tuple-element.10, f32[3,64,128]{2,1,0:T(8,128)S(1)} %get-tuple-element.11, f32[3,64,64]{2,1,0:T(8,128)S(1)} %get-tuple-element.9), kind=kLoop, calls=%fused_computation.10 | loop fusion | flops 9437184 | bytes 12877824 | tf_op jit(solution)/shard_map/vmap()/sub | solution.py:23
  34.7 7.2 %add.77 = f32[3,64,8192]{2,1,0:T(8,128)} reshape(f32[3,64,64,128]{3,2,1,0:T(8,128)} %get-tuple-element.8) | data formatting | bytes 12582912 | tf_op jit(solution)/shard_map/vmap()/add | solution.py:24
  41.8 7.2 %sub.15 = f32[3,64,8192]{2,1,0:T(8,128)} reshape(f32[3,64,64,128]{3,2,1,0:T(8,128)} %get-tuple-element.7) | data formatting | bytes 12582912 | tf_op jit(solution)/shard_map/vmap()/sub | solution.py:23
  49.0 0.6 dynamic-slice.4
  50.3 0.4 concatenate.5
  50.7 6.9 %copy.35 = bf16[6,1,8192]{0,1,2:T(2,128)(2,1)} copy(bf16[6,1,8192]{2,0,1:T(8,128)(2,1)S(1)} %dynamic-slice_bitcast_fusion) | data formatting | bytes 196608 | tf_op jit(solution)/shard_map/reduce_scatter | solution.py:62
  57.6 0.5 broadcast.259
  58.1 45.2 %reduce.1 = bf16[8192,6]{1,0:T(8,128)(2,1)S(1)} reduce(bf16[8192,1,6]{2,1,0:T(2,128)(2,1)} %bitcast.55, bf16[]{:T(256)} %broadcast.259), dimensions={1}, to_apply=%bitcast.51.reduce_sub_computation | reduce | bytes 196610
  103.4 4.1 %reshape.214 = bf16[64,2,384]{2,1,0:T(2,128)(2,1)} reshape(bf16[8192,6]{1,0:T(8,128)(2,1)S(1)} %reduce.1) | data formatting | bytes 196608
  107.5 12.1 %all-to-all-start = ((bf16[64,2,384]{2,1,0:T(2,128)(2,1)}), bf16[64,2,384]{2,1,0:T(2,128)(2,1)S(1)}, u32[]{:S(2)}, u32[]{:S(2)}) async-start(bf16[64,2,384]{2,1,0:T(2,128)(2,1)} %reshape.214), calls=%async_computation | async-start | bytes 196608 | tf_op jit(solution)/shard_map/all_to_all | solution.py:65
  119.6 8.0 %select_convert_fusion.1 = (bf16[3,64,8192]{2,1,0:T(8,128)(2,1)S(1)}, bf16[3,64,8192]{2,1,0:T(8,128)(2,1)}) fusion(f32[3,64,8192]{2,1,0:T(8,128)} %sub.15, f32[64]{0:T(128)S(1)} %get-tuple-element.15, pred[3,8192]{1,0:T(4,128)(4,1)S(1)} %iota_compare_fusion, f32[3,64,8192]{2,1,0:T(8,128)} %add.77, f32[64]{0:T(128)S(1)} %get-tuple-element.16), kind=kLoop, calls=%fused_computation.9 | loop fusion | flops 9437184 | bytes 18899456 | tf_op jit(solution)/shard_map/convert
  127.6 1.6 all-to-all-done
  129.2 8.3 %reshape.215 = bf16[8192,1,6]{2,1,0:T(2,128)(2,1)} reshape(bf16[64,2,384]{2,1,0:T(2,128)(2,1)S(1)} %all-to-all-done) | data formatting | bytes 196608
  137.5 8.1 %copy.36 = bf16[6,1,8192]{2,0,1:T(8,128)(2,1)S(1)} copy(bf16[6,1,8192]{0,1,2:T(2,128)(2,1)} %bitcast.56) | data formatting | bytes 196608 | tf_op jit(solution)/shard_map/all_to_all | solution.py:65
  145.6 0.2 reshape.206
  145.8 6.8 %fusion.6 = bf16[3,128,128]{2,1,0:T(8,128)(2,1)S(1)} fusion(bf16[3,128,8192]{2,1,0:T(8,128)(2,1)} %param.13, bf16[3,128,128]{2,1,0:T(8,128)(2,1)S(1)} %reshape.206, bf16[3,64,8192]{2,1,0:T(8,128)(2,1)} %get-tuple-element.14, bf16[3,64,8192]{2,1,0:T(8,128)(2,1)S(1)} %get-tuple-element.13), kind=kOutput, calls=%fused_computation.12 | convolution fusion | flops 1645264896 | bytes 12779520 | tf_op jit(solution)/shard_map/cnp,crp->cnr/dot_general | solution.py:73
  152.7 18.6 %all_to_all.21 = bf16[6,64,128]{2,0,1:T(8,128)(2,1)S(1)} all-to-all(bf16[6,64,128]{2,0,1:T(8,128)(2,1)S(1)} %copy.38), channel_id=1, replica_groups=mesh['chan'=4,'mset'=8,'blk'=8] {'mset','blk'}, dimensions={1} | all-to-all | bytes 196608 | tf_op jit(solution)/shard_map/all_to_all | solution.py:75
  171.3 0.2 copy.39
  171.5 13.6 %all_gather.3 = bf16[24,1,8192]{2,1,0:T(2,128)(2,1)S(1)} all-gather(bf16[6,1,8192]{2,1,0:T(2,128)(2,1)S(1)} %copy.39), channel_id=1, replica_groups=mesh['chan'=4,'mset'=8,'blk'=8] {'chan'}, dimensions={0}, use_global_device_ids=true | all-gather | bytes 491520 | tf_op jit(solution)/shard_map/all_gather | solution.py:78
  185.1 4.6 %fusion.7 = f32[24,1,384]{2,0,1:T(8,128)S(1)} fusion(bf16[1,384,8192]{2,1,0:T(8,128)(2,1)} %param.12, bf16[24,1,8192]{2,1,0:T(2,128)(2,1)S(1)} %all_gather.3), kind=kOutput, calls=%fused_computation.13 | convolution fusion | flops 150994944 | bytes 6721536 | tf_op jit(solution)/shard_map/ogb,gfb->ogf/dot_general | solution.py:79
  189.8 0.2 fusion.10
  190.0 0.6 copy.41
  (31 shorter events, 0.7 us)
Async XLA Ops:
  0.0 24.4 %copy-start.4 = (s32[12]{0:T(128)S(1)}, s32[12]{0:T(128)}, u32[]{:S(2)}) copy-start(s32[12]{0:T(128)} %param.15) | copy-start | bytes 148
  0.0 24.6 %copy-start.3 = (s32[64]{0:T(128)S(1)}, s32[64]{0:T(128)}, u32[]{:S(2)}) copy-start(s32[64]{0:T(128)} %param.14) | copy-start | bytes 772
  20.8 29.5 %collective-permute-start = (bf16[6,8192]{1,0:T(8,128)(2,1)S(1)}, bf16[6,8192]{1,0:T(8,128)(2,1)S(1)}, u32[]{:S(2)}, u32[]{:S(2)}) collective-permute-start(bf16[6,8192]{1,0:T(8,128)(2,1)S(1)} %slice), channel_id=1, source_target_pairs={{0,64},{64,128},{128,192},{1,65},{65,129},{129,193},{2,66},{66,130... | collective-permute-start | bytes 294920
  41.8 7.2 %copy-start.5 = (u32[256]{0:T(256)S(1)}, u32[256]{0:T(256)}, u32[]{:S(2)}) copy-start(u32[256]{0:T(256)} %constant.68) | copy-start | bytes 3076
  107.5 21.7 %all-to-all-start = ((bf16[64,2,384]{2,1,0:T(2,128)(2,1)}), bf16[64,2,384]{2,1,0:T(2,128)(2,1)S(1)}, u32[]{:S(2)}, u32[]{:S(2)}) async-start(bf16[64,2,384]{2,1,0:T(2,128)(2,1)} %reshape.214), calls=%async_computation | async-start | bytes 196608 | tf_op jit(solution)/shard_map/all_to_all | solution.py:65
  152.6 37.2 %copy-start = (bf16[2,3,1,384]{3,0,2,1:T(2,128)(2,1)S(1)}, bf16[2,3,1,384]{3,0,2,1:T(2,128)(2,1)}, u32[]{:S(2)}) copy-start(bf16[2,3,1,384]{3,0,2,1:T(2,128)(2,1)} %param.8) | copy-start | bytes 13828
  152.6 37.2 %copy-start.1 = (f32[12,3]{0,1:T(4,128)S(1)}, f32[12,3]{0,1:T(4,128)}, u32[]{:S(2)}) copy-start(f32[12,3]{0,1:T(4,128)} %param.9) | copy-start | bytes 436
  152.6 37.2 %copy-start.2 = (f32[3,384]{1,0:T(4,128)S(1)}, f32[3,384]{1,0:T(4,128)}, u32[]{:S(2)}) copy-start(f32[3,384]{1,0:T(4,128)} %param.11) | copy-start | bytes 13828
where the time goes:
time: 192 us; the launch traced here: 191 us
  other arithmetic  65.8 us (34%)
  blocking collectives  46 us (24%)
  local copies, waits for them, and re-layouts  45.2 us (24%)
  starting transfers between devices  15.7 us (8%)
  matrix products  15.3 us (8%)
    unnamed x1, other arithmetic  45.2 us
    all_to_all x1, blocking collectives, on_device(): lax.all_to_all(mode_spectra, ('mset', 'blk'), split_axis=1, concat_axis=2...  18.6 us
    unnamed x20, local copies, waits for them, and re-layouts  14.8 us
    unnamed x1, blocking collectives  13.8 us
    all_gather x1, blocking collectives, on_device(): collected_rows = lax.all_gather(returned, 'chan', axis=0, tiled=True)  13.6 us
    all_to_all x1, starting transfers between devices, on_device(): lax.all_to_all(reduced_sum, ('mset', 'blk'), split_axis=2, concat_axis=1,...  12.1 us
    all_to_all x1, local copies, waits for them, and re-layouts, on_device(): lax.all_to_all(reduced_sum, ('mset', 'blk'), split_axis=2, concat_axis=1,...  8.11 us
    another operation x1, other arithmetic  7.99 us
  transfers between devices with their start and end apart: 2, of which 1 were waited for; matrix products, arithmetic and copies ran while one was open for 17% of the time, Pallas kernels for 0%

commit v1 on v0

--- a/solution.py
+++ b/solution.py
@@ -75,7 +75,14 @@
     returned = lax.all_to_all(
         mode_spectra, ("mset", "blk"), split_axis=1, concat_axis=2, tiled=True
     )
-    collected_rows = lax.all_gather(returned, "chan", axis=0, tiled=True)
+    n_dev = lax.axis_size("chan")
+    route = [(i, (i + 1) % n_dev) for i in range(n_dev)]
+    pieces = [returned]
+    for stride in range(1, n_dev):
+        pieces = [lax.ppermute(pieces[0], "chan", route), *pieces]
+    whole = jnp.concatenate(pieces, axis=0)
+    turn = (lax.axis_index("chan") + 1) * pieces[-1].shape[0]
+    collected_rows = jnp.roll(whole, turn, axis=0)
     harmonic_back = jnp.einsum(
         "ogb,gfb->ogf", collected_rows, legendre, preferred_element_type=jnp.float32
     )

time: 192 us -> 198 us (1.031)
  waiting for transfers between devices: 1.63 us -> 20.1 us
  blocking collectives: 46 us -> 32.4 us
    ppermute x0 -> x3, waiting for transfers between devices: none -> 18.5 us  [on_device(): pieces = [lax.ppermute(pieces[0], 'chan', route), *pieces]]
    all_gather x1 -> x0, blocking collectives: 13.6 us -> none  [on_device(): collected_rows = lax.all_gather(returned, 'chan', axis=0, tiled=True)]
  transfers between devices with their start and end apart: 2 -> 5, of which waited for: 1 -> 4; matrix products, arithmetic and copies ran while one was open for 17% -> 17% of each run, Pallas kernels for 0% -> 0%
where the time goes in v1:
time: 198 us; the launch traced here: 197 us
  other arithmetic  65.8 us (33%)
  local copies, waits for them, and re-layouts  46.7 us (24%)
  blocking collectives  32.4 us (16%)
  waiting for transfers between devices  20.1 us (10%)
  starting transfers between devices  15.7 us (8%)
  matrix products  15.2 us (8%)
    unnamed x1, other arithmetic  45.2 us
    all_to_all x1, blocking collectives, on_device(): lax.all_to_all(mode_spectra, ('mset', 'blk'), split_axis=1, concat_axis=2...  18.6 us
    ppermute x3, waiting for transfers between devices, on_device(): pieces = [lax.ppermute(pieces[0], 'chan', route), *pieces]  18.5 us
    unnamed x20, local copies, waits for them, and re-layouts  14.8 us
    unnamed x1, blocking collectives  13.8 us
    all_to_all x1, starting transfers between devices, on_device(): lax.all_to_all(reduced_sum, ('mset', 'blk'), split_axis=2, concat_axis=1,...  12.1 us
    all_to_all x1, local copies, waits for them, and re-layouts, on_device(): lax.all_to_all(reduced_sum, ('mset', 'blk'), split_axis=2, concat_axis=1,...  8.11 us
    another operation x1, other arithmetic  7.97 us
  transfers between devices with their start and end apart: 5, of which 4 were waited for; matrix products, arithmetic and copies ran while one was open for 17% of the time, Pallas kernels for 0%

profile of v1, /device:TPU:8, one launch (start us, length us, event | category | flops | bytes accessed | tf_op | source)
XLA Modules:
  0.0 196.9 jit_solution(14186186511561413064)
XLA Ops:
  0.0 0.7 fusion.28
  0.7 0.7 convert_bitcast_fusion
  1.4 0.8 copy.32
  2.3 0.8 compare_select_fusion
  3.2 3.7 %fusion.1 = bf16[24,1,8192]{2,0,1:T(8,128)(2,1)S(1)} fusion(bf16[24,384]{1,0:T(8,128)(2,1)S(1)} %convert_element_type.71, bf16[1,384,8192]{2,1,0:T(8,128)(2,1)} %param.12), kind=kOutput, calls=%fused_computation.2 | convolution fusion | flops 151191552 | bytes 6703104 | tf_op jit(solution)/shard_map/ijn,jnw->ijw/dot_general | solution.py:59
  6.9 13.8 %fusion = bf16[8,8192]{1,0:T(8,128)(2,1)S(1)} fusion(bf16[24,1,8192]{2,0,1:T(8,128)(2,1)S(1)} %fusion.1), kind=kCustom, calls=%all-reduce-scatter | all-reduce-scatter fusion | flops 262145 | bytes 525312
  20.8 3.6 %collective-permute-start.3 = (bf16[6,8192]{1,0:T(8,128)(2,1)S(1)}, bf16[6,8192]{1,0:T(8,128)(2,1)S(1)}, u32[]{:S(2)}, u32[]{:S(2)}) collective-permute-start(bf16[6,8192]{1,0:T(8,128)(2,1)S(1)} %slice), channel_id=1, source_target_pairs={{0,64},{64,128},{128,192},{1,65},{65,129},{129,193},{2,66},{66,130... | collective-permute-start | bytes 294920
  24.8 1.4 fusion.16
  26.2 1.4 fusion.20
  27.6 7.1 %multiply_subtract_fusion = (f32[3,64,64,128]{3,2,1,0:T(8,128)}, f32[3,64,64,128]{3,2,1,0:T(8,128)}) fusion(f32[3,64,128]{2,1,0:T(8,128)S(1)} %get-tuple-element.12, f32[3,64,64]{2,1,0:T(8,128)S(1)} %get-tuple-element.10, f32[3,64,128]{2,1,0:T(8,128)S(1)} %get-tuple-element.11, f32[3,64,64]{2,1,0:T(8,128)S(1)} %get-tuple-element.9), kind=kLoop, calls=%fused_computation.10 | loop fusion | flops 9437184 | bytes 12877824 | tf_op jit(solution)/shard_map/vmap()/sub | solution.py:23
  34.6 7.2 %add.90 = f32[3,64,8192]{2,1,0:T(8,128)} reshape(f32[3,64,64,128]{3,2,1,0:T(8,128)} %get-tuple-element.8) | data formatting | bytes 12582912 | tf_op jit(solution)/shard_map/vmap()/add | solution.py:24
  41.8 7.2 %sub.19 = f32[3,64,8192]{2,1,0:T(8,128)} reshape(f32[3,64,64,128]{3,2,1,0:T(8,128)} %get-tuple-element.7) | data formatting | bytes 12582912 | tf_op jit(solution)/shard_map/vmap()/sub | solution.py:23
  49.0 0.6 dynamic-slice.4
  50.3 0.4 concatenate.12
  50.7 6.9 %copy.34 = bf16[6,1,8192]{0,1,2:T(2,128)(2,1)} copy(bf16[6,1,8192]{2,0,1:T(8,128)(2,1)S(1)} %dynamic-slice_bitcast_fusion) | data formatting | bytes 196608 | tf_op jit(solution)/shard_map/reduce_scatter | solution.py:62
  57.6 0.5 broadcast.259
  58.1 45.2 %reduce.1 = bf16[8192,6]{1,0:T(8,128)(2,1)S(1)} reduce(bf16[8192,1,6]{2,1,0:T(2,128)(2,1)} %bitcast.55, bf16[]{:T(256)} %broadcast.259), dimensions={1}, to_apply=%bitcast.51.reduce_sub_computation | reduce | bytes 196610
  103.3 4.1 %reshape.214 = bf16[64,2,384]{2,1,0:T(2,128)(2,1)} reshape(bf16[8192,6]{1,0:T(8,128)(2,1)S(1)} %reduce.1) | data formatting | bytes 196608
  107.5 12.1 %all-to-all-start = ((bf16[64,2,384]{2,1,0:T(2,128)(2,1)}), bf16[64,2,384]{2,1,0:T(2,128)(2,1)S(1)}, u32[]{:S(2)}, u32[]{:S(2)}) async-start(bf16[64,2,384]{2,1,0:T(2,128)(2,1)} %reshape.214), calls=%async_computation | async-start | bytes 196608 | tf_op jit(solution)/shard_map/all_to_all | solution.py:65
  119.6 8.0 %select_convert_fusion.1 = (bf16[3,64,8192]{2,1,0:T(8,128)(2,1)S(1)}, bf16[3,64,8192]{2,1,0:T(8,128)(2,1)}) fusion(f32[3,64,8192]{2,1,0:T(8,128)} %sub.19, f32[64]{0:T(128)S(1)} %get-tuple-element.15, pred[3,8192]{1,0:T(4,128)(4,1)S(1)} %iota_compare_fusion, f32[3,64,8192]{2,1,0:T(8,128)} %add.90, f32[64]{0:T(128)S(1)} %get-tuple-element.16), kind=kLoop, calls=%fused_computation.9 | loop fusion | flops 9437184 | bytes 18899456 | tf_op jit(solution)/shard_map/convert
  127.6 1.6 all-to-all-done
  129.2 8.3 %reshape.215 = bf16[8192,1,6]{2,1,0:T(2,128)(2,1)} reshape(bf16[64,2,384]{2,1,0:T(2,128)(2,1)S(1)} %all-to-all-done) | data formatting | bytes 196608
  137.4 8.1 %copy.35 = bf16[6,1,8192]{2,0,1:T(8,128)(2,1)S(1)} copy(bf16[6,1,8192]{0,1,2:T(2,128)(2,1)} %bitcast.56) | data formatting | bytes 196608 | tf_op jit(solution)/shard_map/all_to_all | solution.py:65
  145.7 6.8 %fusion.6 = bf16[3,128,128]{2,1,0:T(8,128)(2,1)S(1)} fusion(bf16[3,128,8192]{2,1,0:T(8,128)(2,1)} %param.13, bf16[3,128,128]{2,1,0:T(8,128)(2,1)S(1)} %reshape.206, bf16[3,64,8192]{2,1,0:T(8,128)(2,1)} %get-tuple-element.14, bf16[3,64,8192]{2,1,0:T(8,128)(2,1)S(1)} %get-tuple-element.13), kind=kOutput, calls=%fused_computation.12 | convolution fusion | flops 1645264896 | bytes 12779520 | tf_op jit(solution)/shard_map/cnp,crp->cnr/dot_general | solution.py:73
  152.6 18.6 %all_to_all.21 = bf16[6,64,128]{2,0,1:T(8,128)(2,1)S(1)} all-to-all(bf16[6,64,128]{2,0,1:T(8,128)(2,1)S(1)} %copy.37), channel_id=1, replica_groups=mesh['chan'=4,'mset'=8,'blk'=8] {'mset','blk'}, dimensions={1} | all-to-all | bytes 196608 | tf_op jit(solution)/shard_map/all_to_all | solution.py:75
  171.2 6.2 %collective-permute-done = bf16[6,1,8192]{2,0,1:T(8,128)(2,1)S(1)} collective-permute-done((bf16[6,1,8192]{2,0,1:T(8,128)(2,1)S(1)}, bf16[6,1,8192]{2,0,1:T(8,128)(2,1)S(1)}, u32[]{:S(2)}, u32[]{:S(2)}) %collective-permute-start) | collective-permute-done | bytes 98336 | tf_op jit(solution)/shard_map/ppermute | solution.py:82
  177.4 6.2 %collective-permute-done.1 = bf16[6,1,8192]{2,0,1:T(8,128)(2,1)S(1)} collective-permute-done((bf16[6,1,8192]{2,0,1:T(8,128)(2,1)S(1)}, bf16[6,1,8192]{2,0,1:T(8,128)(2,1)S(1)}, u32[]{:S(2)}, u32[]{:S(2)}) %collective-permute-start.1) | collective-permute-done | bytes 98336 | tf_op jit(solution)/shard_map/ppermute | solution.py:82
  183.6 6.2 %collective-permute-done.2 = bf16[6,1,8192]{2,0,1:T(8,128)(2,1)S(1)} collective-permute-done((bf16[6,1,8192]{2,0,1:T(8,128)(2,1)S(1)}, bf16[6,1,8192]{2,0,1:T(8,128)(2,1)S(1)}, u32[]{:S(2)}, u32[]{:S(2)}) %collective-permute-start.2) | collective-permute-done | bytes 98336 | tf_op jit(solution)/shard_map/ppermute | solution.py:82
  189.8 1.6 concatenate.11
  191.4 4.5 %fusion.7 = f32[24,1,384]{2,0,1:T(8,128)S(1)} fusion(bf16[1,384,8192]{2,1,0:T(8,128)(2,1)} %param.12, bf16[48,1,8192]{2,0,1:T(8,128)(2,1)S(1)} %concatenate.11, s32[]{:T(128)S(6)} %select_n.75), kind=kOutput, calls=%fused_computation.13 | convolution fusion | flops 150994944 | bytes 6721540 | tf_op jit(solution)/shard_map/ogb,gfb->ogf/dot_general | solution.py:86
  196.1 0.2 fusion.10
  196.3 0.6 copy.39
  (36 shorter events, 1.0 us)
Async XLA Ops:
  0.0 24.4 %copy-start.4 = (s32[12]{0:T(128)S(1)}, s32[12]{0:T(128)}, u32[]{:S(2)}) copy-start(s32[12]{0:T(128)} %param.15) | copy-start | bytes 148
  0.0 24.6 %copy-start.3 = (s32[64]{0:T(128)S(1)}, s32[64]{0:T(128)}, u32[]{:S(2)}) copy-start(s32[64]{0:T(128)} %param.14) | copy-start | bytes 772
  20.8 29.5 %collective-permute-start.3 = (bf16[6,8192]{1,0:T(8,128)(2,1)S(1)}, bf16[6,8192]{1,0:T(8,128)(2,1)S(1)}, u32[]{:S(2)}, u32[]{:S(2)}) collective-permute-start(bf16[6,8192]{1,0:T(8,128)(2,1)S(1)} %slice), channel_id=1, source_target_pairs={{0,64},{64,128},{128,192},{1,65},{65,129},{129,193},{2,66},{66,130... | collective-permute-start | bytes 294920
  41.8 7.2 %copy-start.5 = (u32[256]{0:T(256)S(1)}, u32[256]{0:T(256)}, u32[]{:S(2)}) copy-start(u32[256]{0:T(256)} %constant.89) | copy-start | bytes 3076
  107.5 21.7 %all-to-all-start = ((bf16[64,2,384]{2,1,0:T(2,128)(2,1)}), bf16[64,2,384]{2,1,0:T(2,128)(2,1)S(1)}, u32[]{:S(2)}, u32[]{:S(2)}) async-start(bf16[64,2,384]{2,1,0:T(2,128)(2,1)} %reshape.214), calls=%async_computation | async-start | bytes 196608 | tf_op jit(solution)/shard_map/all_to_all | solution.py:65
  152.5 43.6 %copy-start = (bf16[2,3,1,384]{3,0,2,1:T(2,128)(2,1)S(1)}, bf16[2,3,1,384]{3,0,2,1:T(2,128)(2,1)}, u32[]{:S(2)}) copy-start(bf16[2,3,1,384]{3,0,2,1:T(2,128)(2,1)} %param.8) | copy-start | bytes 13828
  152.5 43.5 %copy-start.1 = (f32[12,3]{0,1:T(4,128)S(1)}, f32[12,3]{0,1:T(4,128)}, u32[]{:S(2)}) copy-start(f32[12,3]{0,1:T(4,128)} %param.9) | copy-start | bytes 436
  152.5 43.5 %copy-start.2 = (f32[3,384]{1,0:T(4,128)S(1)}, f32[3,384]{1,0:T(4,128)}, u32[]{:S(2)}) copy-start(f32[3,384]{1,0:T(4,128)} %param.11) | copy-start | bytes 13828
  171.2 6.2 %collective-permute-start = (bf16[6,1,8192]{2,0,1:T(8,128)(2,1)S(1)}, bf16[6,1,8192]{2,0,1:T(8,128)(2,1)S(1)}, u32[]{:S(2)}, u32[]{:S(2)}) collective-permute-start(bf16[6,1,8192]{2,0,1:T(8,128)(2,1)S(1)} %bitcast.57), channel_id=1, source_target_pairs={{0,64},{64,128},{128,192},{192,0},{1,65},{65,129},{129,193},{193,1... | collective-permute-start | bytes 294920 | tf_op jit(solution)/shard_map/ppermute | solution.py:82
  177.4 6.2 %collective-permute-start.1 = (bf16[6,1,8192]{2,0,1:T(8,128)(2,1)S(1)}, bf16[6,1,8192]{2,0,1:T(8,128)(2,1)S(1)}, u32[]{:S(2)}, u32[]{:S(2)}) collective-permute-start(bf16[6,1,8192]{2,0,1:T(8,128)(2,1)S(1)} %collective-permute-done), channel_id=1, source_target_pairs={{0,64},{64,128},{128,192},{192,0},{1,65},{65,129},{129,193},{193,1... | collective-permute-start | bytes 294920 | tf_op jit(solution)/shard_map/ppermute | solution.py:82
  183.6 6.2 %collective-permute-start.2 = (bf16[6,1,8192]{2,0,1:T(8,128)(2,1)S(1)}, bf16[6,1,8192]{2,0,1:T(8,128)(2,1)S(1)}, u32[]{:S(2)}, u32[]{:S(2)}) collective-permute-start(bf16[6,1,8192]{2,0,1:T(8,128)(2,1)S(1)} %collective-permute-done.1), channel_id=1, source_target_pairs={{0,64},{64,128},{128,192},{192,0},{1,65},{65,129},{129,193},{193,1... | collective-permute-start | bytes 294920 | tf_op jit(solution)/shard_map/ppermute | solution.py:82
